TPU v7x, 32 devices: a whole 2x2x4 slice. The times are simulated.
32 devices in a mesh: dom: 8 (over z, y), sub: 4 (over x, core).
Axes of the slice: x: 2, y: 2, z: 4, core: 2. Of those that a mesh axis runs over, the one named last changes fastest.
Arguments:
- nodes: bfloat16 [16384, 128], P(('dom', 'sub')), may hold values from -6 to 6
- edges: bfloat16 [65536, 128], P(('dom', 'sub')), may hold values from -6 to 6
- senders: int32 [65536], P(('dom', 'sub')), may hold values from 0 to 895
- receivers: int32 [65536], P(('dom', 'sub')), may hold values from 0 to 511
- edge_live: int32 [65536], P(('dom', 'sub')), may hold values from 0 to 1, as said below
- outlet_flags: int32 [16384], P(('dom', 'sub')), may hold values 0 or 1
- send_rows: int32 [12288], P(('dom', 'sub')), may hold values from 0 to 511
- edge_first: float32 [3, 384, 128], replicated, may hold values from -0.3125 to 0.3125
- edge_bias: float32 [3, 128], replicated, may hold values from -3 to 3
- edge_second: float32 [3, 128, 128], replicated, may hold values from -0.5 to 0.5
- edge_offset: float32 [3, 128], replicated, may hold values from -3 to 3
- edge_gain: float32 [3, 128], replicated, may hold values from 0.25 to 1.75
- node_first: float32 [3, 256, 128], replicated, may hold values from -0.375 to 0.375
- node_bias: float32 [3, 128], replicated, may hold values from -3 to 3
- node_second: float32 [3, 128, 128], replicated, may hold values from -0.5 to 0.5
- node_offset: float32 [3, 128], replicated, may hold values from -3 to 3
- node_gain: float32 [3, 128], replicated, may hold values from 0.25 to 1.75
- outlet_map: float32 [3, 128, 128], replicated, may hold values from -0.5 to 0.5
- grad_out: float32 [16384, 128], P(('dom', 'sub')), may hold values from -6 to 6
Outputs:
- latent_out: float32 [16384, 128], P(('dom', 'sub'))
- latent_grad: float32 [16384, 128], P(('dom', 'sub'))
- edge_first_grad: float32 [3, 384, 128], replicated
- edge_bias_grad: float32 [3, 128], replicated
- edge_second_grad: float32 [3, 128, 128], replicated
- edge_offset_grad: float32 [3, 128], replicated
- edge_gain_grad: float32 [3, 128], replicated
- node_first_grad: float32 [3, 256, 128], replicated
- node_bias_grad: float32 [3, 128], replicated
- node_second_grad: float32 [3, 128, 128], replicated
- node_offset_grad: float32 [3, 128], replicated
- node_gain_grad: float32 [3, 128], replicated
- outlet_map_grad: float32 [3, 128, 128], replicated
Inputs may be any that keep to these rules, and one draw needn't show every extreme that they name: `edge_live`: on each device the live edge slots are the first ones of its 2048; each device has between a quarter and all of them live, and some device has all live. `senders`: indices below 512 name the device's own nodes; higher ones name halo rows.
All inputs are finite; a program needn't handle non-finite values. No bound on the sum of `outlet_flags` on one device may be relied on, other than what follows from the above.
Results may differ from a plain program's by a relative error of at most 0.018.
Values may be sent and summed in bfloat16 or wider, within the bound.
A program may use at most 320 MiB of HBM per device.

v0:
```python
import jax
import jax.numpy as jnp
from jax import lax
from jax.sharding import PartitionSpec as P


def passed_along(value, axis, steps):
    count = lax.axis_size(axis)
    first, last = (max(0, -steps), min(count, count - steps))
    return lax.ppermute(value, axis, [(source, source + steps) for source in range(first, last)])


def normalize(values):
    mean = jnp.mean(values, axis=-1, keepdims=True)
    centered = values - mean
    variance = jnp.mean(centered * centered, axis=-1, keepdims=True)
    return centered * lax.rsqrt(variance + 1e-05)


def layer_local(latent, edge_state, halo, layer_weights, senders, receivers, live, flags):
    (
        edge_first,
        edge_bias,
        edge_second,
        edge_offset,
        edge_gain,
        node_first,
        node_bias,
        node_second,
        node_offset,
        node_gain,
        outlet_map,
    ) = layer_weights
    own = latent.astype(jnp.bfloat16)
    extended = jnp.concatenate([own, halo], axis=0)
    joined = jnp.concatenate(
        [edge_state.astype(jnp.bfloat16), extended[senders], own[receivers]], axis=1
    )
    act_one = jax.nn.silu(
        jnp.dot(joined, edge_first.astype(jnp.bfloat16), preferred_element_type=jnp.float32)
        + edge_bias
    ).astype(jnp.bfloat16)
    pre_two = (
        jnp.dot(act_one, edge_second.astype(jnp.bfloat16), preferred_element_type=jnp.float32)
        + edge_offset
    )
    message = live[:, None] * (edge_gain * normalize(pre_two))
    new_edge = edge_state + message
    summed = jax.ops.segment_sum(message, receivers, num_segments=latent.shape[0])
    summed_half = summed.astype(jnp.bfloat16)
    node_in = jnp.concatenate([own, summed_half], axis=1)
    node_hidden = jax.nn.silu(
        jnp.dot(node_in, node_first.astype(jnp.bfloat16), preferred_element_type=jnp.float32)
        + node_bias
    ).astype(jnp.bfloat16)
    update = node_gain * normalize(
        jnp.dot(node_hidden, node_second.astype(jnp.bfloat16), preferred_element_type=jnp.float32)
        + node_offset
    )
    outlet = flags[:, None] * jnp.dot(
        summed_half, outlet_map.astype(jnp.bfloat16), preferred_element_type=jnp.float32
    )
    return (latent + update + outlet, new_edge)


def send_halo(latent, send_rows, low, high):
    sent = latent[send_rows].astype(jnp.bfloat16)
    from_lower = passed_along(sent[low : 2 * low], "sub", 1)
    from_upper = passed_along(sent[:low], "sub", -1)
    dom_lower = passed_along(sent[2 * low + high :], "dom", 1)
    dom_upper = passed_along(sent[2 * low : 2 * low + high], "dom", -1)
    return jnp.concatenate([from_lower, from_upper, dom_lower, dom_upper], axis=0)


def return_halo(halo_grad, send_rows, low, high, shape):
    back_high = passed_along(halo_grad[:low], "sub", -1)
    back_low = passed_along(halo_grad[low : 2 * low], "sub", 1)
    dom_back_high = passed_along(halo_grad[2 * low : 2 * low + high], "dom", -1)
    dom_back_low = passed_along(halo_grad[2 * low + high :], "dom", 1)
    returned = jnp.concatenate([back_low, back_high, dom_back_low, dom_back_high], axis=0).astype(
        jnp.float32
    )
    return jnp.zeros(shape, jnp.float32).at[send_rows].add(returned)


def flatten_all(grads):
    return jnp.concatenate([grad.reshape(-1) for grad in grads])


def unflatten_all(flat, shapes):
    pieces = []
    offset = 0
    for shape in shapes:
        length = 1
        for extent in shape:
            length = length * extent
        pieces.append(flat[offset : offset + length].reshape(shape))
        offset = offset + length
    return pieces


def on_device(
    nodes,
    edges,
    senders,
    receivers,
    edge_live,
    outlet_flags,
    send_rows,
    edge_first,
    edge_bias,
    edge_second,
    edge_offset,
    edge_gain,
    node_first,
    node_bias,
    node_second,
    node_offset,
    node_gain,
    outlet_map,
    grad_out,
):
    weights = (
        edge_first,
        edge_bias,
        edge_second,
        edge_offset,
        edge_gain,
        node_first,
        node_bias,
        node_second,
        node_offset,
        node_gain,
        outlet_map,
    )
    layers = edge_first.shape[0]
    low = nodes.shape[0] // 8
    high = nodes.shape[0] // 4
    live = edge_live.astype(jnp.float32)
    flags = outlet_flags.astype(jnp.float32)
    latent = nodes.astype(jnp.float32)
    edge_state = edges.astype(jnp.float32)

    def advance(latent_in, edge_in, halo, layer_weights):
        return layer_local(latent_in, edge_in, halo, layer_weights, senders, receivers, live, flags)

    saved = []
    for layer in range(layers):
        layer_weights = tuple((weight[layer] for weight in weights))
        halo = send_halo(latent, send_rows, low, high)
        (latent, edge_state), pullback = jax.vjp(advance, latent, edge_state, halo, layer_weights)
        saved.append(pullback)
    layer_shapes = [weight.shape[1:] for weight in weights]
    latent_grad = grad_out
    edge_grad = jnp.zeros_like(edge_state)
    per_layer = [None] * layers
    for layer in reversed(range(layers)):
        pullback = saved[layer]
        latent_grad, edge_grad, halo_grad, weight_grads = pullback((latent_grad, edge_grad))
        latent_grad = latent_grad + return_halo(halo_grad, send_rows, low, high, latent_grad.shape)
        flat = flatten_all(weight_grads)
        per_layer[layer] = flat
    stacked = jnp.stack(per_layer, axis=0)
    stacked = lax.psum(stacked, ("dom", "sub"))
    by_layer = [unflatten_all(stacked[layer], layer_shapes) for layer in range(layers)]
    results = [
        jnp.stack([by_layer[layer][which] for layer in range(layers)], axis=0)
        for which in range(len(weights))
    ]
    return (
        latent,
        latent_grad,
        results[0],
        results[1],
        results[2],
        results[3],
        results[4],
        results[5],
        results[6],
        results[7],
        results[8],
        results[9],
        results[10],
    )


def solution(mesh):
    placed = (
        P(("dom", "sub"), None),
        P(("dom", "sub"), None),
        P(("dom", "sub")),
        P(("dom", "sub")),
        P(("dom", "sub")),
        P(("dom", "sub")),
        P(("dom", "sub")),
        P(),
        P(),
        P(),
        P(),
        P(),
        P(),
        P(),
        P(),
        P(),
        P(),
        P(),
        P(("dom", "sub"), None),
    )
    return jax.shard_map(
        on_device,
        mesh=mesh,
        in_specs=placed,
        out_specs=(
            P(("dom", "sub"), None),
            P(("dom", "sub"), None),
            P(),
            P(),
            P(),
            P(),
            P(),
            P(),
            P(),
            P(),
            P(),
            P(),
            P(),
        ),
        check_vma=False,
    )
```

profile of v0, /device:TPU:0, one launch (start us, length us, event | category | flops | bytes accessed | tf_op | source)
XLA Modules:
  0.0 548.7 jit_solution(7893833300528265434)
XLA Ops:
  12.7 3.8 collective-permute-start
  18.4 6.1 %collective-permute-start.2 = (bf16[128,128]{1,0:T(8,128)(2,1)}, bf16[128,128]{1,0:T(8,128)(2,1)}, u32[]{:S(2)}, u32[]{:S(2)}) collective-permute-start(bf16[128,128]{1,0:T(8,128)(2,1)} %get-tuple-element.114), channel_id=1, source_target_pairs={{0,4},{4,8},{8,12},{12,16},{16,20},{20,24},{24,28},{1,5},{5,9},{9,... | collective-permute-start | bytes 98312 | tf_op jit(solution)/shard_map/ppermute | solution.py:10
  33.6 6.2 %gather_fusion.2 = bf16[2048,128]{1,0:T(8,128)(2,1)S(1)} fusion(bf16[512,128]{1,0:T(8,128)(2,1)S(1)} %copy-done, s32[2048]{0:T(1024)S(1)} %get-tuple-element.118), kind=kCustom, calls=%fused_computation.2 | custom fusion | bytes 1056768 | tf_op jit(solution)/shard_map/jvp()/gather | solution.py:37
  42.0 6.2 %gather_fusion.1 = bf16[2048,128]{1,0:T(8,128)(2,1)S(1)} fusion(bf16[896,128]{1,0:T(8,128)(2,1)S(1)} %constant_dynamic-update-slice_fusion, s32[2048]{0:T(1024)S(1)} %get-tuple-element.121), kind=kCustom, calls=%fused_computation.1 | custom fusion | bytes 1056768 | tf_op jit(solution)/shard_map/jvp()/gather | solution.py:37
  53.7 11.9 %scatter_custom_fusion = f32[512,128]{1,0:T(8,128)S(1)} fusion(s32[2048]{0:T(1024)S(1)} %copy-done.84, f32[2048,128]{1,0:T(8,128)} %copy.74, f32[]{:T(128)} %constant.51.clone.1), kind=kCustom, calls=%fused_computation.256 | custom fusion | flops 262144 | bytes 262656 | tf_op jit(solution)/shard_map/jvp()/scatter-add | solution.py:49
  71.2 5.5 collective-permute-start.6
  78.6 3.2 collective-permute-start.4
  82.0 6.2 %gather_fusion.5 = bf16[2048,128]{1,0:T(8,128)(2,1)S(1)} fusion(bf16[512,128]{1,0:T(8,128)(2,1)S(1)} %copy.80, s32[2048]{0:T(1024)S(1)} %copy-done.66), kind=kCustom, calls=%fused_computation.5 | custom fusion | bytes 1056768 | tf_op jit(solution)/shard_map/jvp()/gather | solution.py:37
  91.0 6.2 %gather_fusion.4 = bf16[2048,128]{1,0:T(8,128)(2,1)S(1)} fusion(bf16[896,128]{1,0:T(8,128)(2,1)S(1)} %copy.79, s32[2048]{0:T(1024)S(1)} %copy-done.60), kind=kCustom, calls=%fused_computation.4 | custom fusion | bytes 1056768 | tf_op jit(solution)/shard_map/jvp()/gather | solution.py:37
  98.2 2.0 convolution_add_fusion.3
  104.0 2.6 copy.83
  106.6 11.9 %scatter_custom_fusion.1 = f32[512,128]{1,0:T(8,128)S(1)} fusion(s32[2048]{0:T(1024)S(1)} %copy-done.85, f32[2048,128]{1,0:T(8,128)} %copy.83, f32[]{:T(128)} %constant.51.clone.1), kind=kCustom, calls=%fused_computation.254 | custom fusion | flops 262144 | bytes 262656 | tf_op jit(solution)/shard_map/jvp()/scatter-add | solution.py:49
  126.5 4.4 collective-permute-start.8
  132.2 5.3 collective-permute-start.10
  137.7 7.2 %gather_fusion.8 = bf16[2048,128]{1,0:T(8,128)(2,1)S(1)} fusion(bf16[512,128]{1,0:T(8,128)(2,1)S(1)} %copy.89, s32[2048]{0:T(1024)} %copy-done.65), kind=kCustom, calls=%fused_computation.8 | custom fusion | bytes 1056768 | tf_op jit(solution)/shard_map/jvp()/gather | solution.py:37
  147.1 7.2 %gather_fusion.7 = bf16[2048,128]{1,0:T(8,128)(2,1)S(1)} fusion(bf16[896,128]{1,0:T(8,128)(2,1)S(1)} %copy.88, s32[2048]{0:T(1024)} %copy-done.59), kind=kCustom, calls=%fused_computation.7 | custom fusion | bytes 1056768 | tf_op jit(solution)/shard_map/jvp()/gather | solution.py:37
  155.2 2.0 convolution_add_fusion.1
  161.1 2.5 copy.92
  163.6 12.9 %scatter_custom_fusion.2 = f32[512,128]{1,0:T(8,128)} fusion(s32[2048]{0:T(1024)} %param.22, f32[2048,128]{1,0:T(8,128)} %copy.92, f32[]{:T(128)} %constant.51.clone.1), kind=kCustom, calls=%fused_computation.252 | custom fusion | flops 262144 | bytes 262656 | tf_op jit(solution)/shard_map/jvp()/scatter-add | solution.py:49
  176.5 1.7 copy.93
  178.2 1.8 fusion.37
  185.7 1.7 fusion.192
  190.0 8.4 %gather_fusion.9 = f32[2048,128]{1,0:T(8,128)} fusion(f32[512,128]{1,0:T(8,128)S(1)} %fusion.19, s32[2048]{0:T(1024)} %get-tuple-element.119), kind=kCustom, calls=%fused_computation.9 | custom fusion | bytes 2105344 | tf_op jit(solution)/shard_map/transpose(jvp())/gather | solution.py:49
  198.3 2.6 copy.97
  200.9 2.2 multiply_reduce_fusion
  205.5 2.0 fusion.191
  212.5 11.9 %scatter_custom_fusion.3 = bf16[896,128]{1,0:T(8,128)(2,1)S(1)} fusion(s32[2048]{0:T(1024)} %get-tuple-element.120, bf16[2048,128]{1,0:T(8,128)(2,1)} %copy.99, bf16[]{:T(256)} %constant.59.clone.1), kind=kCustom, calls=%fused_computation.261 | custom fusion | flops 262144 | bytes 229888 | tf_op jit(solution)/shard_map/transpose(jvp())/scatter-add | solution.py:37
  226.9 3.4 collective-permute-start.12
  231.6 4.6 collective-permute-start.14
  237.4 11.9 %scatter_fusion = bf16[512,128]{1,0:T(8,128)(2,1)S(1)} fusion(bf16[512,128]{1,0:T(8,128)(2,1)S(1)} %slice_add_fusion.2, s32[2048]{0:T(1024)} %get-tuple-element.117, bf16[2048,128]{1,0:T(8,128)(2,1)S(1)} %copy.100), kind=kCustom, calls=%fused_computation.16 | custom fusion | flops 262144 | bytes 1581056 | tf_op jit(solution)/shard_map/transpose(jvp())/scatter-add | solution.py:37
  254.9 1.6 constant_dynamic-update-slice_fusion.25
  264.3 3.6 stack.26
  267.9 3.2 scatter_custom_fusion.5
  272.7 1.9 fusion.43
  274.6 1.6 fusion.194
  279.9 7.6 %gather_fusion.10 = f32[2048,128]{1,0:T(8,128)} fusion(f32[512,128]{1,0:T(8,128)S(1)} %fusion.21, s32[2048]{0:T(1024)S(1)} %copy-done.70), kind=kCustom, calls=%fused_computation.10 | custom fusion | bytes 2105344 | tf_op jit(solution)/shard_map/transpose(jvp())/gather | solution.py:49
  287.6 1.6 copy.103
  289.2 2.0 multiply_reduce_fusion.1
  291.3 1.6 fusion.161
  294.7 2.0 fusion.193
  301.4 11.9 %scatter_custom_fusion.6 = bf16[896,128]{1,0:T(8,128)(2,1)S(1)} fusion(s32[2048]{0:T(1024)} %get-tuple-element.120, bf16[2048,128]{1,0:T(8,128)(2,1)} %copy.105, bf16[]{:T(256)} %constant.59.clone.1), kind=kCustom, calls=%fused_computation.259 | custom fusion | flops 262144 | bytes 229888 | tf_op jit(solution)/shard_map/transpose(jvp())/scatter-add | solution.py:37
  315.9 11.8 %scatter_fusion.1 = bf16[512,128]{1,0:T(8,128)(2,1)S(1)} fusion(bf16[512,128]{1,0:T(8,128)(2,1)S(1)} %slice_add_fusion.1, s32[2048]{0:T(1024)} %get-tuple-element.117, bf16[2048,128]{1,0:T(8,128)(2,1)S(1)} %copy.106), kind=kCustom, calls=%fused_computation.19 | custom fusion | flops 262144 | bytes 1581056 | tf_op jit(solution)/shard_map/transpose(jvp())/scatter-add | solution.py:37
  328.7 2.7 collective-permute-start.16
  332.8 4.3 collective-permute-start.18
  344.0 1.6 constant_dynamic-update-slice_fusion.24
  352.6 3.6 stack.25
  356.2 2.9 scatter_custom_fusion.8
  362.8 1.6 fusion.196
  368.5 8.4 %gather_fusion.11 = f32[2048,128]{1,0:T(8,128)} fusion(f32[512,128]{1,0:T(8,128)S(1)} %fusion.23, s32[2048]{0:T(1024)} %get-tuple-element.119), kind=kCustom, calls=%fused_computation.11 | custom fusion | bytes 2105344 | tf_op jit(solution)/shard_map/transpose(jvp())/gather | solution.py:49
  376.9 2.6 copy.109
  379.5 2.0 multiply_reduce_fusion.2
  385.4 1.6 convolution_convert_fusion
  387.2 2.5 stack.24
  389.7 2.4 pad_maximum_fusion
  392.2 11.9 %scatter_custom_fusion.9 = bf16[896,128]{1,0:T(8,128)(2,1)S(1)} fusion(s32[2048]{0:T(1024)} %get-tuple-element.120, bf16[2048,384]{1,0:T(8,128)(2,1)S(1)} %convolution_convert_fusion, bf16[]{:T(256)} %constant.59.clone.1), kind=kCustom, calls=%fused_computation.171 | custom fusion | flops 262144 | bytes 754176 | tf_op jit(solution)/shard_map/transpose(jvp())/scatter-add | solution.py:37
  404.1 12.0 %scatter_custom_fusion.10 = bf16[512,128]{1,0:T(8,128)(2,1)S(1)} fusion(bf16[512,128]{1,0:T(8,128)(2,1)S(1)} %slice_add_fusion, s32[2048]{0:T(1024)} %get-tuple-element.117, bf16[2048,384]{1,0:T(8,128)(2,1)S(1)} %convolution_convert_fusion), kind=kCustom, calls=%fused_computation.169 | custom fusion | flops 262144 | bytes 655360 | tf_op jit(solution)/shard_map/transpose(jvp())/scatter-add | solution.py:37
  416.1 4.0 collective-permute-start.20
  421.4 4.3 collective-permute-start.22
  427.3 4.2 collective-permute-done.23
  431.5 2.9 scatter_custom_fusion.11
  434.4 96.1 %all-reduce.2.cloned.1.call-done = f32[3,131840]{1,0:T(4,128)} async-done(((f32[3,131840]{1,0:T(4,128)}), f32[3,131840]{1,0:T(4,128)}) %all-reduce.2.cloned.1.call-update) | async-done | bytes 1582096 | tf_op jit(solution)/shard_map/psum | solution.py:164
  530.5 1.7 fusion.167
  533.1 2.3 fusion.165
  536.1 2.4 fusion.168
  (491 shorter events, 138.4 us)
Async XLA Ops:
  7.2 22.1 %copy-start = (bf16[512,128]{1,0:T(8,128)(2,1)S(1)}, bf16[512,128]{1,0:T(8,128)(2,1)}, u32[]{:S(2)}) copy-start(bf16[512,128]{1,0:T(8,128)(2,1)} %param.19) | copy-start | bytes 393220
  7.2 17.3 %copy-start.105 = (f32[3,128]{1,0:T(4,128)S(1)}, f32[3,128]{1,0:T(4,128)}, u32[]{:S(2)}) copy-start(f32[3,128]{1,0:T(4,128)} %param.27) | copy-start | bytes 4612
  7.2 17.9 %copy-start.106 = (f32[3,128]{1,0:T(4,128)S(1)}, f32[3,128]{1,0:T(4,128)}, u32[]{:S(2)}) copy-start(f32[3,128]{1,0:T(4,128)} %param.29) | copy-start | bytes 4612
  7.2 18.4 %copy-start.107 = (f32[3,128]{1,0:T(4,128)S(1)}, f32[3,128]{1,0:T(4,128)}, u32[]{:S(2)}) copy-start(f32[3,128]{1,0:T(4,128)} %param.30) | copy-start | bytes 4612
  7.2 19.0 %copy-start.108 = (f32[3,128]{1,0:T(4,128)S(1)}, f32[3,128]{1,0:T(4,128)}, u32[]{:S(2)}) copy-start(f32[3,128]{1,0:T(4,128)} %param.32) | copy-start | bytes 4612
  7.2 19.5 %copy-start.109 = (f32[3,128]{1,0:T(4,128)S(1)}, f32[3,128]{1,0:T(4,128)}, u32[]{:S(2)}) copy-start(f32[3,128]{1,0:T(4,128)} %param.34) | copy-start | bytes 4612
  7.2 20.1 %copy-start.110 = (f32[3,128]{1,0:T(4,128)S(1)}, f32[3,128]{1,0:T(4,128)}, u32[]{:S(2)}) copy-start(f32[3,128]{1,0:T(4,128)} %param.35) | copy-start | bytes 4612
  7.3 20.7 %copy-start.95 = (s32[2048]{0:T(1024)S(1)}, s32[2048]{0:T(1024)}, u32[]{:S(2)}) copy-start(s32[2048]{0:T(1024)} %param.21) | copy-start | bytes 24580
  7.3 21.3 %copy-start.84 = (s32[2048]{0:T(1024)S(1)}, s32[2048]{0:T(1024)}, u32[]{:S(2)}) copy-start(s32[2048]{0:T(1024)} %param.22) | copy-start | bytes 24580
  7.3 21.9 %copy-start.18 = (bf16[2048,128]{1,0:T(8,128)(2,1)S(1)}, bf16[2048,128]{1,0:T(8,128)(2,1)}, u32[]{:S(2)}) copy-start(bf16[2048,128]{1,0:T(8,128)(2,1)} %param.20) | copy-start | bytes 1572868
  7.3 523.3 %all-reduce.2.cloned.1.call-start = ((), (), s32[]{:S(2)}) async-start(), calls=%async_computation | async-start | bytes 4218880 | tf_op jit(solution)/shard_map/psum | solution.py:164
  8.1 22.2 %copy-start.96 = (s32[384]{0:T(512)}, s32[384]{0:T(512)S(1)}, u32[]{:S(2)}) copy-start(s32[384]{0:T(512)S(1)} %compare_select_fusion.2) | copy-start | bytes 4612
  9.1 19.4 %copy-start.23 = (bf16[512,128]{0,1:T(8,128)(2,1)}, bf16[512,128]{0,1:T(8,128)(2,1)S(1)}, u32[]{:S(2)}) copy-start(bf16[512,128]{0,1:T(8,128)(2,1)S(1)} %copy.72) | copy-start | bytes 393220
  9.3 21.0 %copy-start.104 = (s32[512]{0:T(512)S(1)}, s32[512]{0:T(512)}, u32[]{:S(2)}) copy-start(s32[512]{0:T(512)} %param.24) | copy-start | bytes 6148
  9.3 21.0 %copy-start.97 = (s32[2048]{0:T(1024)S(1)}, s32[2048]{0:T(1024)}, u32[]{:S(2)}) copy-start(s32[2048]{0:T(1024)} %param.23) | copy-start | bytes 24580
  9.3 21.0 %copy-start.56 = (f32[3,128,128]{2,1,0:T(8,128)S(1)}, f32[3,128,128]{2,1,0:T(8,128)}, u32[]{:S(2)}) copy-start(f32[3,128,128]{2,1,0:T(8,128)} %param.28) | copy-start | bytes 589828
  10.8 20.2 %copy-start.57 = (f32[3,128,128]{2,1,0:T(8,128)S(1)}, f32[3,128,128]{2,1,0:T(8,128)}, u32[]{:S(2)}) copy-start(f32[3,128,128]{2,1,0:T(8,128)} %param.33) | copy-start | bytes 589828
  11.4 29.1 %collective-permute-start.1 = (bf16[64,128]{1,0:T(8,128)(2,1)}, bf16[64,128]{1,0:T(8,128)(2,1)}, u32[]{:S(2)}, u32[]{:S(2)}) collective-permute-start(bf16[64,128]{1,0:T(8,128)(2,1)} %get-tuple-element.115), channel_id=1, source_target_pairs={{1,0},{2,1},{3,2},{5,4},{6,5},{7,6},{9,8},{10,9},{11,10},{13,12},{... | collective-permute-start | bytes 49160 | tf_op jit(solution)/shard_map/ppermute | solution.py:10
  12.7 19.0 %copy-start.58 = (f32[3,128,128]{2,1,0:T(8,128)S(1)}, f32[3,128,128]{2,1,0:T(8,128)}, u32[]{:S(2)}) copy-start(f32[3,128,128]{2,1,0:T(8,128)} %param.36) | copy-start | bytes 589828
  12.7 27.1 %collective-permute-start = (bf16[64,128]{1,0:T(8,128)(2,1)}, bf16[64,128]{1,0:T(8,128)(2,1)}, u32[]{:S(2)}, u32[]{:S(2)}) collective-permute-start(bf16[64,128]{1,0:T(8,128)(2,1)} %get-tuple-element.116), channel_id=1, source_target_pairs={{0,1},{1,2},{2,3},{4,5},{5,6},{6,7},{8,9},{9,10},{10,11},{12,13},{... | collective-permute-start | bytes 49160 | tf_op jit(solution)/shard_map/ppermute | solution.py:10
  17.1 24.9 %collective-permute-start.3 = (bf16[128,128]{1,0:T(8,128)(2,1)}, bf16[128,128]{1,0:T(8,128)(2,1)S(1)}, u32[]{:S(2)}, u32[]{:S(2)}) collective-permute-start(bf16[128,128]{1,0:T(8,128)(2,1)} %get-tuple-element.113), channel_id=1, source_target_pairs={{4,0},{8,4},{12,8},{16,12},{20,16},{24,20},{28,24},{5,1},{9,5},{13... | collective-permute-start | bytes 98312 | tf_op jit(solution)/shard_map/ppermute | solution.py:10
  18.4 22.8 %collective-permute-start.2 = (bf16[128,128]{1,0:T(8,128)(2,1)}, bf16[128,128]{1,0:T(8,128)(2,1)}, u32[]{:S(2)}, u32[]{:S(2)}) collective-permute-start(bf16[128,128]{1,0:T(8,128)(2,1)} %get-tuple-element.114), channel_id=1, source_target_pairs={{0,4},{4,8},{8,12},{12,16},{16,20},{20,24},{24,28},{1,5},{5,9},{9,... | collective-permute-start | bytes 98312 | tf_op jit(solution)/shard_map/ppermute | solution.py:10
  32.3 33.3 %copy-start.41 = (bf16[3,256,128]{2,1,0:T(8,128)(2,1)}, bf16[3,256,128]{2,1,0:T(8,128)(2,1)S(1)}, u32[]{:S(2)}) copy-start(bf16[3,256,128]{2,1,0:T(8,128)(2,1)S(1)} %convert.42) | copy-start | bytes 589828
  33.5 15.0 %copy-start.19 = (bf16[3,384,128]{2,1,0:T(8,128)(2,1)}, bf16[3,384,128]{2,1,0:T(8,128)(2,1)S(1)}, u32[]{:S(2)}) copy-start(bf16[3,384,128]{2,1,0:T(8,128)(2,1)S(1)} %convert.40) | copy-start | bytes 884740
  67.0 14.9 %copy-start.78 = (f32[512]{0:T(512)}, f32[512]{0:T(512)S(1)}, u32[]{:S(2)}) copy-start(f32[512]{0:T(512)S(1)} %broadcast_multiply_fusion.5) | copy-start | bytes 6148
  67.0 14.9 %copy-start.66 = (s32[2048]{0:T(1024)S(1)}, s32[2048]{0:T(1024)}, u32[]{:S(2)}) copy-start(s32[2048]{0:T(1024)} %copy-done.65) | copy-start | bytes 24580
  67.1 21.1 %copy-start.88 = (f32[512]{0:T(512)}, f32[512]{0:T(512)S(1)}, u32[]{:S(2)}) copy-start(f32[512]{0:T(512)S(1)} %multiply_reduce_fusion.17) | copy-start | bytes 6148
  67.1 21.1 %copy-start.81 = (f32[512]{0:T(512)}, f32[512]{0:T(512)S(1)}, u32[]{:S(2)}) copy-start(f32[512]{0:T(512)S(1)} %fusion.145) | copy-start | bytes 6148
  68.2 21.7 %copy-start.25 = (bf16[512,128]{0,1:T(8,128)(2,1)}, bf16[512,128]{0,1:T(8,128)(2,1)S(1)}, u32[]{:S(2)}) copy-start(bf16[512,128]{0,1:T(8,128)(2,1)S(1)} %get-tuple-element.144) | copy-start | bytes 393220
  69.9 19.4 %collective-permute-start.7 = (bf16[128,128]{0,1:T(8,128)(2,1)S(1)}, bf16[128,128]{0,1:T(8,128)(2,1)}, u32[]{:S(2)}, u32[]{:S(2)}) collective-permute-start(bf16[128,128]{0,1:T(8,128)(2,1)S(1)} %get-tuple-element.109), channel_id=1, source_target_pairs={{4,0},{8,4},{12,8},{16,12},{20,16},{24,20},{28,24},{5,1},{9,5},{13... | collective-permute-start | bytes 98312 | tf_op jit(solution)/shard_map/ppermute | solution.py:10
  71.2 18.7 %collective-permute-start.6 = (bf16[128,128]{0,1:T(8,128)(2,1)S(1)}, bf16[128,128]{0,1:T(8,128)(2,1)}, u32[]{:S(2)}, u32[]{:S(2)}) collective-permute-start(bf16[128,128]{0,1:T(8,128)(2,1)S(1)} %get-tuple-element.110), channel_id=1, source_target_pairs={{0,4},{4,8},{8,12},{12,16},{16,20},{20,24},{24,28},{1,5},{5,9},{9,... | collective-permute-start | bytes 98312 | tf_op jit(solution)/shard_map/ppermute | solution.py:10
  77.3 12.0 %collective-permute-start.5 = (bf16[64,128]{0,1:T(8,128)(2,1)}, bf16[64,128]{0,1:T(8,128)(2,1)S(1)}, u32[]{:S(2)}, u32[]{:S(2)}) collective-permute-start(bf16[64,128]{0,1:T(8,128)(2,1)} %get-tuple-element.111), channel_id=1, source_target_pairs={{1,0},{2,1},{3,2},{5,4},{6,5},{7,6},{9,8},{10,9},{11,10},{13,12},{... | collective-permute-start | bytes 49160 | tf_op jit(solution)/shard_map/ppermute | solution.py:10
  78.6 10.7 %collective-permute-start.4 = (bf16[64,128]{0,1:T(8,128)(2,1)S(1)}, bf16[64,128]{0,1:T(8,128)(2,1)S(1)}, u32[]{:S(2)}, u32[]{:S(2)}) collective-permute-start(bf16[64,128]{0,1:T(8,128)(2,1)S(1)} %get-tuple-element.112), channel_id=1, source_target_pairs={{0,1},{1,2},{2,3},{4,5},{5,6},{6,7},{8,9},{9,10},{10,11},{12,13},{... | collective-permute-start | bytes 49160 | tf_op jit(solution)/shard_map/ppermute | solution.py:10
  104.0 14.6 %copy-start.26 = (bf16[512,128]{0,1:T(8,128)(2,1)S(1)}, bf16[512,128]{0,1:T(8,128)(2,1)}, u32[]{:S(2)}) copy-start(bf16[512,128]{0,1:T(8,128)(2,1)} %copy-done.25) | copy-start | bytes 393220
  104.0 14.6 %copy-start.114 = (f32[128]{0:T(128)S(1)}, f32[128]{0:T(128)}, u32[]{:S(2)}) copy-start(f32[128]{0:T(128)} %get-tuple-element.127) | copy-start | bytes 1540
  104.0 15.8 %copy-start.115 = (f32[128]{0:T(128)S(1)}, f32[128]{0:T(128)}, u32[]{:S(2)}) copy-start(f32[128]{0:T(128)} %get-tuple-element.130) | copy-start | bytes 1540
  120.9 16.6 %copy-start.38 = (f32[512,128]{1,0:T(8,128)S(1)}, f32[512,128]{1,0:T(8,128)}, u32[]{:S(2)}) copy-start(f32[512,128]{1,0:T(8,128)} %param.37) | copy-start | bytes 786436
  121.0 16.6 %copy-start.89 = (f32[512]{0:T(512)}, f32[512]{0:T(512)S(1)}, u32[]{:S(2)}) copy-start(f32[512]{0:T(512)S(1)} %multiply_reduce_fusion.16) | copy-start | bytes 6148
  122.1 22.8 %copy-start.13 = (f32[512,128]{0,1:T(8,128)}, f32[512,128]{0,1:T(8,128)S(1)}, u32[]{:S(2)}) copy-start(f32[512,128]{0,1:T(8,128)S(1)} %get-tuple-element.151) | copy-start | bytes 786436
  122.1 23.8 %copy-start.30 = (bf16[512,128]{0,1:T(8,128)(2,1)}, bf16[512,128]{0,1:T(8,128)(2,1)S(1)}, u32[]{:S(2)}) copy-start(bf16[512,128]{0,1:T(8,128)(2,1)S(1)} %get-tuple-element.150) | copy-start | bytes 393220
  125.2 20.8 %collective-permute-start.9 = (bf16[64,128]{0,1:T(8,128)(2,1)}, bf16[64,128]{0,1:T(8,128)(2,1)}, u32[]{:S(2)}, u32[]{:S(2)}) collective-permute-start(bf16[64,128]{0,1:T(8,128)(2,1)} %get-tuple-element.107), channel_id=1, source_target_pairs={{1,0},{2,1},{3,2},{5,4},{6,5},{7,6},{9,8},{10,9},{11,10},{13,12},{... | collective-permute-start | bytes 49160 | tf_op jit(solution)/shard_map/ppermute | solution.py:10
  126.5 19.5 %collective-permute-start.8 = (bf16[64,128]{0,1:T(8,128)(2,1)}, bf16[64,128]{0,1:T(8,128)(2,1)}, u32[]{:S(2)}, u32[]{:S(2)}) collective-permute-start(bf16[64,128]{0,1:T(8,128)(2,1)} %get-tuple-element.108), channel_id=1, source_target_pairs={{0,1},{1,2},{2,3},{4,5},{5,6},{6,7},{8,9},{9,10},{10,11},{12,13},{... | collective-permute-start | bytes 49160 | tf_op jit(solution)/shard_map/ppermute | solution.py:10
  130.9 15.1 %collective-permute-start.11 = (bf16[128,128]{0,1:T(8,128)(2,1)}, bf16[128,128]{0,1:T(8,128)(2,1)}, u32[]{:S(2)}, u32[]{:S(2)}) collective-permute-start(bf16[128,128]{0,1:T(8,128)(2,1)} %get-tuple-element.105), channel_id=1, source_target_pairs={{4,0},{8,4},{12,8},{16,12},{20,16},{24,20},{28,24},{5,1},{9,5},{13... | collective-permute-start | bytes 98312 | tf_op jit(solution)/shard_map/ppermute | solution.py:10
  132.2 13.8 %collective-permute-start.10 = (bf16[128,128]{0,1:T(8,128)(2,1)}, bf16[128,128]{0,1:T(8,128)(2,1)}, u32[]{:S(2)}, u32[]{:S(2)}) collective-permute-start(bf16[128,128]{0,1:T(8,128)(2,1)} %get-tuple-element.106), channel_id=1, source_target_pairs={{0,4},{4,8},{8,12},{12,16},{16,20},{20,24},{24,28},{1,5},{5,9},{9,... | collective-permute-start | bytes 98312 | tf_op jit(solution)/shard_map/ppermute | solution.py:10
  137.6 46.4 %copy-start.5 = (f32[512,128]{0,1:T(8,128)}, f32[512,128]{0,1:T(8,128)S(1)}, u32[]{:S(2)}) copy-start(f32[512,128]{0,1:T(8,128)S(1)} %copy.95) | copy-start | bytes 786436
  226.9 41.0 %collective-permute-start.12 = (bf16[64,128]{1,0:T(8,128)(2,1)}, bf16[64,128]{1,0:T(8,128)(2,1)}, u32[]{:S(2)}, u32[]{:S(2)}) collective-permute-start(bf16[64,128]{1,0:T(8,128)(2,1)} %get-tuple-element.101), channel_id=1, source_target_pairs={{0,1},{1,2},{2,3},{4,5},{5,6},{6,7},{8,9},{9,10},{10,11},{12,13},{... | collective-permute-start | bytes 49160 | tf_op jit(solution)/shard_map/ppermute | solution.py:10
  230.3 37.6 %collective-permute-start.13 = (bf16[64,128]{1,0:T(8,128)(2,1)}, bf16[64,128]{1,0:T(8,128)(2,1)}, u32[]{:S(2)}, u32[]{:S(2)}) collective-permute-start(bf16[64,128]{1,0:T(8,128)(2,1)} %get-tuple-element.102), channel_id=1, source_target_pairs={{1,0},{2,1},{3,2},{5,4},{6,5},{7,6},{9,8},{10,9},{11,10},{13,12},{... | collective-permute-start | bytes 49160 | tf_op jit(solution)/shard_map/ppermute | solution.py:10
  231.6 36.3 %collective-permute-start.14 = (bf16[128,128]{1,0:T(8,128)(2,1)}, bf16[128,128]{1,0:T(8,128)(2,1)}, u32[]{:S(2)}, u32[]{:S(2)}) collective-permute-start(bf16[128,128]{1,0:T(8,128)(2,1)} %get-tuple-element.103), channel_id=1, source_target_pairs={{0,4},{4,8},{8,12},{12,16},{16,20},{20,24},{24,28},{1,5},{5,9},{9,... | collective-permute-start | bytes 98312 | tf_op jit(solution)/shard_map/ppermute | solution.py:10
  236.1 31.8 %collective-permute-start.15 = (bf16[128,128]{1,0:T(8,128)(2,1)}, bf16[128,128]{1,0:T(8,128)(2,1)}, u32[]{:S(2)}, u32[]{:S(2)}) collective-permute-start(bf16[128,128]{1,0:T(8,128)(2,1)} %get-tuple-element.104), channel_id=1, source_target_pairs={{4,0},{8,4},{12,8},{16,12},{20,16},{24,20},{28,24},{5,1},{9,5},{13... | collective-permute-start | bytes 98312 | tf_op jit(solution)/shard_map/ppermute | solution.py:10
  237.4 26.1 %copy-start.32 = (f32[512,128]{0,1:T(8,128)S(1)}, f32[512,128]{0,1:T(8,128)}, u32[]{:S(2)}) copy-start(f32[512,128]{0,1:T(8,128)} %fusion.3) | copy-start | bytes 786436
  249.4 21.9 %copy-start.12 = (f32[512,128]{0,1:T(8,128)S(1)}, f32[512,128]{0,1:T(8,128)}, u32[]{:S(2)}) copy-start(f32[512,128]{0,1:T(8,128)} %copy-done.11) | copy-start | bytes 786436
  249.4 21.9 %copy-start.80 = (f32[512]{0:T(512)S(1)}, f32[512]{0:T(512)}, u32[]{:S(2)}) copy-start(f32[512]{0:T(512)} %copy-done.79) | copy-start | bytes 6148
  249.4 21.9 %copy-start.83 = (f32[512]{0:T(512)S(1)}, f32[512]{0:T(512)}, u32[]{:S(2)}) copy-start(f32[512]{0:T(512)} %copy-done.82) | copy-start | bytes 6148
  249.4 21.9 %copy-start.99 = (f32[128]{0:T(128)S(1)}, f32[128]{0:T(128)}, u32[]{:S(2)}) copy-start(f32[128]{0:T(128)} %get-tuple-element.124) | copy-start | bytes 1540
  327.7 31.5 %copy-start.10 = (f32[512,128]{0,1:T(8,128)S(1)}, f32[512,128]{0,1:T(8,128)}, u32[]{:S(2)}) copy-start(f32[512,128]{0,1:T(8,128)} %copy-done.9) | copy-start | bytes 786436
  328.7 27.4 %collective-permute-start.16 = (bf16[64,128]{1,0:T(8,128)(2,1)}, bf16[64,128]{1,0:T(8,128)(2,1)S(1)}, u32[]{:S(2)}, u32[]{:S(2)}) collective-permute-start(bf16[64,128]{1,0:T(8,128)(2,1)} %get-tuple-element.97), channel_id=1, source_target_pairs={{0,1},{1,2},{2,3},{4,5},{5,6},{6,7},{8,9},{9,10},{10,11},{12,13},{... | collective-permute-start | bytes 49160 | tf_op jit(solution)/shard_map/ppermute | solution.py:10
  331.5 24.7 %collective-permute-start.17 = (bf16[64,128]{1,0:T(8,128)(2,1)}, bf16[64,128]{1,0:T(8,128)(2,1)S(1)}, u32[]{:S(2)}, u32[]{:S(2)}) collective-permute-start(bf16[64,128]{1,0:T(8,128)(2,1)} %get-tuple-element.98), channel_id=1, source_target_pairs={{1,0},{2,1},{3,2},{5,4},{6,5},{7,6},{9,8},{10,9},{11,10},{13,12},{... | collective-permute-start | bytes 49160 | tf_op jit(solution)/shard_map/ppermute | solution.py:10
  332.8 23.4 %collective-permute-start.18 = (bf16[128,128]{1,0:T(8,128)(2,1)}, bf16[128,128]{1,0:T(8,128)(2,1)S(1)}, u32[]{:S(2)}, u32[]{:S(2)}) collective-permute-start(bf16[128,128]{1,0:T(8,128)(2,1)} %get-tuple-element.99), channel_id=1, source_target_pairs={{0,4},{4,8},{8,12},{12,16},{16,20},{20,24},{24,28},{1,5},{5,9},{9,... | collective-permute-start | bytes 98312 | tf_op jit(solution)/shard_map/ppermute | solution.py:10
  337.1 19.1 %collective-permute-start.19 = (bf16[128,128]{1,0:T(8,128)(2,1)}, bf16[128,128]{1,0:T(8,128)(2,1)S(1)}, u32[]{:S(2)}, u32[]{:S(2)}) collective-permute-start(bf16[128,128]{1,0:T(8,128)(2,1)} %get-tuple-element.100), channel_id=1, source_target_pairs={{4,0},{8,4},{12,8},{16,12},{20,16},{24,20},{28,24},{5,1},{9,5},{13... | collective-permute-start | bytes 98312 | tf_op jit(solution)/shard_map/ppermute | solution.py:10
  416.1 11.0 %collective-permute-start.20 = (bf16[64,128]{1,0:T(8,128)(2,1)S(1)}, bf16[64,128]{1,0:T(8,128)(2,1)S(1)}, u32[]{:S(2)}, u32[]{:S(2)}) collective-permute-start(bf16[64,128]{1,0:T(8,128)(2,1)S(1)} %get-tuple-element.93), channel_id=1, source_target_pairs={{0,1},{1,2},{2,3},{4,5},{5,6},{6,7},{8,9},{9,10},{10,11},{12,13},{... | collective-permute-start | bytes 49160 | tf_op jit(solution)/shard_map/ppermute | solution.py:10
  420.1 6.9 %collective-permute-start.21 = (bf16[64,128]{1,0:T(8,128)(2,1)S(1)}, bf16[64,128]{1,0:T(8,128)(2,1)S(1)}, u32[]{:S(2)}, u32[]{:S(2)}) collective-permute-start(bf16[64,128]{1,0:T(8,128)(2,1)S(1)} %get-tuple-element.94), channel_id=1, source_target_pairs={{1,0},{2,1},{3,2},{5,4},{6,5},{7,6},{9,8},{10,9},{11,10},{13,12},{... | collective-permute-start | bytes 49160 | tf_op jit(solution)/shard_map/ppermute | solution.py:10
  421.4 5.9 %collective-permute-start.22 = (bf16[128,128]{1,0:T(8,128)(2,1)S(1)}, bf16[128,128]{1,0:T(8,128)(2,1)S(1)}, u32[]{:S(2)}, u32[]{:S(2)}) collective-permute-start(bf16[128,128]{1,0:T(8,128)(2,1)S(1)} %get-tuple-element.95), channel_id=1, source_target_pairs={{0,4},{4,8},{8,12},{12,16},{16,20},{20,24},{24,28},{1,5},{5,9},{9,... | collective-permute-start | bytes 98312 | tf_op jit(solution)/shard_map/ppermute | solution.py:10
  425.7 5.8 %collective-permute-start.23 = (bf16[128,128]{1,0:T(8,128)(2,1)S(1)}, bf16[128,128]{1,0:T(8,128)(2,1)S(1)}, u32[]{:S(2)}, u32[]{:S(2)}) collective-permute-start(bf16[128,128]{1,0:T(8,128)(2,1)S(1)} %get-tuple-element.96), channel_id=1, source_target_pairs={{4,0},{8,4},{12,8},{16,12},{20,16},{24,20},{28,24},{5,1},{9,5},{13... | collective-permute-start | bytes 98312 | tf_op jit(solution)/shard_map/ppermute | solution.py:10
  434.4 101.7 %copy-start.49 = (f32[512,128]{1,0:T(8,128)}, f32[512,128]{1,0:T(8,128)S(1)}, u32[]{:S(2)}) copy-start(f32[512,128]{1,0:T(8,128)S(1)} %scatter_custom_fusion.11) | copy-start | bytes 786436
  (92 other events, 311.6 us)
Sparse Core Ops, SparseCore 0:
  392.3 138.2 all-reduce.1
where the time goes:
time: 559 us; the launch traced here: 549 us
  local copies, waits for them, and re-layouts  161 us (29%)
  other arithmetic  151 us (27%)
  waiting for transfers between devices  101 us (18%)
  starting transfers between devices  67.2 us (12%)
  matrix products  52.3 us (9%)
  between operations  16.9 us (3%)
    psum x1, waiting for transfers between devices, on_device(): stacked = lax.psum(stacked, ('dom', 'sub'))  96.1 us
    ppermute x24, starting transfers between devices, passed_along(): lax.ppermute(value, axis, [(source, source + steps) for source in range(f...  67.2 us
    scatter-add x3, other arithmetic, layer_local(): jax.ops.segment_sum(message, receivers, num_segments=latent.shape[0])  36.7 us
    unnamed x299, local copies, waits for them, and re-layouts  36.6 us
    scatter-add x3, other arithmetic, layer_local(): extended[senders]  35.8 us
    scatter-add x3, other arithmetic, layer_local(): own[receivers]  35.6 us
    gather x6, local copies, waits for them, and re-layouts, layer_local(): jax.ops.segment_sum(message, receivers, num_segments=latent.shape[0])  31 us
    gather x5, local copies, waits for them, and re-layouts, layer_local(): extended[senders]  21.6 us
  transfers between devices with their start and end apart: 25, of which 3 were waited for; matrix products, arithmetic and copies ran while one was open for 20% of the time, Pallas kernels for 0%

commit v1 on v0

--- a/solution.py
+++ b/solution.py
@@ -2,6 +2,11 @@
 import jax.numpy as jnp
 from jax import lax
 from jax.sharding import PartitionSpec as P
+
+
+def _prepare_values(panel):
+    v_now = lax.psum(lax.psum(panel, axis_name="sub"), axis_name="dom")
+    return v_now
 
 
 def passed_along(value, axis, steps):
@@ -161,7 +166,7 @@
         flat = flatten_all(weight_grads)
         per_layer[layer] = flat
     stacked = jnp.stack(per_layer, axis=0)
-    stacked = lax.psum(stacked, ("dom", "sub"))
+    stacked = _prepare_values(stacked)
     by_layer = [unflatten_all(stacked[layer], layer_shapes) for layer in range(layers)]
     results = [
         jnp.stack([by_layer[layer][which] for layer in range(layers)], axis=0)

time: 559 us -> 581 us (1.039)
  waiting for transfers between devices: 101 us -> 125 us
    psum x1 -> x2, waiting for transfers between devices: 96.1 us -> 120 us  [_prepare_values(): v_now = lax.psum(lax.psum(panel, axis_name='sub'), axis_name='dom')]
    unnamed x299 -> x317, local copies, waits for them, and re-layouts: 36.6 us -> 36 us
  transfers between devices with their start and end apart: 25 -> 26, of which waited for: 3 -> 4; matrix products, arithmetic and copies ran while one was open for 20% -> 20% of each run, Pallas kernels for 0% -> 0%
where the time goes in v1:
time: 581 us; the launch traced here: 571 us
  local copies, waits for them, and re-layouts  162 us (28%)
  other arithmetic  151 us (26%)
  waiting for transfers between devices  125 us (22%)
  starting transfers between devices  63.6 us (11%)
  matrix products  52.2 us (9%)
  between operations  17.1 us (3%)
    psum x2, waiting for transfers between devices, _prepare_values(): v_now = lax.psum(lax.psum(panel, axis_name='sub'), axis_name='dom')  120 us
    ppermute x24, starting transfers between devices, passed_along(): lax.ppermute(value, axis, [(source, source + steps) for source in range(f...  63.3 us
    scatter-add x3, other arithmetic, layer_local(): jax.ops.segment_sum(message, receivers, num_segments=latent.shape[0])  36.7 us
    unnamed x317, local copies, waits for them, and re-layouts  36 us
    scatter-add x3, other arithmetic, layer_local(): extended[senders]  35.6 us
    scatter-add x3, other arithmetic, layer_local(): own[receivers]  35.1 us
    gather x6, local copies, waits for them, and re-layouts, layer_local(): jax.ops.segment_sum(message, receivers, num_segments=latent.shape[0])  30.9 us
    gather x5, local copies, waits for them, and re-layouts, layer_local(): own[receivers]  22.7 us
  transfers between devices with their start and end apart: 26, of which 4 were waited for; matrix products, arithmetic and copies ran while one was open for 20% of the time, Pallas kernels for 0%

profile of v1, /device:TPU:0, one launch (start us, length us, event | category | flops | bytes accessed | tf_op | source)
XLA Modules:
  0.0 570.6 jit_solution(12645345929435236009)
XLA Ops:
  12.7 3.6 collective-permute-start
  18.2 6.1 %collective-permute-start.2 = (bf16[128,128]{1,0:T(8,128)(2,1)}, bf16[128,128]{1,0:T(8,128)(2,1)}, u32[]{:S(2)}, u32[]{:S(2)}) collective-permute-start(bf16[128,128]{1,0:T(8,128)(2,1)} %get-tuple-element.114), channel_id=1, source_target_pairs={{0,4},{4,8},{8,12},{12,16},{16,20},{20,24},{24,28},{1,5},{5,9},{9,... | collective-permute-start | bytes 98312 | tf_op jit(solution)/shard_map/ppermute | solution.py:15
  31.4 1.6 convert.44
  34.2 7.3 %gather_fusion.2 = bf16[2048,128]{1,0:T(8,128)(2,1)S(1)} fusion(bf16[512,128]{1,0:T(8,128)(2,1)S(1)} %copy-done, s32[2048]{0:T(1024)} %get-tuple-element.118), kind=kCustom, calls=%fused_computation.2 | custom fusion | bytes 1056768 | tf_op jit(solution)/shard_map/jvp()/gather | solution.py:42
  44.6 6.2 %gather_fusion.1 = bf16[2048,128]{1,0:T(8,128)(2,1)S(1)} fusion(bf16[896,128]{1,0:T(8,128)(2,1)S(1)} %constant_dynamic-update-slice_fusion, s32[2048]{0:T(1024)S(1)} %copy-done.61), kind=kCustom, calls=%fused_computation.1 | custom fusion | bytes 1056768 | tf_op jit(solution)/shard_map/jvp()/gather | solution.py:42
  56.2 11.9 %scatter_custom_fusion = f32[512,128]{1,0:T(8,128)S(1)} fusion(s32[2048]{0:T(1024)} %param.22, f32[2048,128]{1,0:T(8,128)} %copy.74, f32[]{:T(128)} %constant.51.clone.1), kind=kCustom, calls=%fused_computation.256 | custom fusion | flops 262144 | bytes 262656 | tf_op jit(solution)/shard_map/jvp()/scatter-add | solution.py:54
  73.7 5.5 collective-permute-start.6
  81.0 3.2 collective-permute-start.4
  84.4 6.2 %gather_fusion.5 = bf16[2048,128]{1,0:T(8,128)(2,1)S(1)} fusion(bf16[512,128]{1,0:T(8,128)(2,1)S(1)} %copy.80, s32[2048]{0:T(1024)S(1)} %copy-done.67), kind=kCustom, calls=%fused_computation.5 | custom fusion | bytes 1056768 | tf_op jit(solution)/shard_map/jvp()/gather | solution.py:42
  93.5 6.2 %gather_fusion.4 = bf16[2048,128]{1,0:T(8,128)(2,1)S(1)} fusion(bf16[896,128]{1,0:T(8,128)(2,1)S(1)} %copy.79, s32[2048]{0:T(1024)S(1)} %copy-done.62), kind=kCustom, calls=%fused_computation.4 | custom fusion | bytes 1056768 | tf_op jit(solution)/shard_map/jvp()/gather | solution.py:42
  100.7 2.0 convolution_add_fusion.3
  106.5 2.6 copy.83
  109.1 11.9 %scatter_custom_fusion.1 = f32[512,128]{1,0:T(8,128)S(1)} fusion(s32[2048]{0:T(1024)S(1)} %copy-done.92, f32[2048,128]{1,0:T(8,128)} %copy.83, f32[]{:T(128)} %constant.51.clone.1), kind=kCustom, calls=%fused_computation.254 | custom fusion | flops 262144 | bytes 262656 | tf_op jit(solution)/shard_map/jvp()/scatter-add | solution.py:54
  128.9 4.4 collective-permute-start.8
  134.7 5.3 collective-permute-start.10
  140.2 7.2 %gather_fusion.8 = bf16[2048,128]{1,0:T(8,128)(2,1)S(1)} fusion(bf16[512,128]{1,0:T(8,128)(2,1)S(1)} %copy.89, s32[2048]{0:T(1024)} %get-tuple-element.118), kind=kCustom, calls=%fused_computation.8 | custom fusion | bytes 1056768 | tf_op jit(solution)/shard_map/jvp()/gather | solution.py:42
  149.5 7.2 %gather_fusion.7 = bf16[2048,128]{1,0:T(8,128)(2,1)S(1)} fusion(bf16[896,128]{1,0:T(8,128)(2,1)S(1)} %copy.88, s32[2048]{0:T(1024)} %get-tuple-element.121), kind=kCustom, calls=%fused_computation.7 | custom fusion | bytes 1056768 | tf_op jit(solution)/shard_map/jvp()/gather | solution.py:42
  157.7 2.0 convolution_add_fusion.1
  163.6 2.5 copy.92
  166.1 12.9 %scatter_custom_fusion.2 = f32[512,128]{1,0:T(8,128)} fusion(s32[2048]{0:T(1024)} %param.22, f32[2048,128]{1,0:T(8,128)} %copy.92, f32[]{:T(128)} %constant.51.clone.1), kind=kCustom, calls=%fused_computation.252 | custom fusion | flops 262144 | bytes 262656 | tf_op jit(solution)/shard_map/jvp()/scatter-add | solution.py:54
  179.0 1.7 copy.93
  180.7 1.7 fusion.37
  187.3 1.6 fusion.192
  191.9 8.3 %gather_fusion.9 = f32[2048,128]{1,0:T(8,128)} fusion(f32[512,128]{1,0:T(8,128)S(1)} %fusion.19, s32[2048]{0:T(1024)} %get-tuple-element.119), kind=kCustom, calls=%fused_computation.9 | custom fusion | bytes 2105344 | tf_op jit(solution)/shard_map/transpose(jvp())/gather | solution.py:54
  200.2 2.6 copy.97
  202.9 2.3 multiply_reduce_fusion
  214.0 11.9 %scatter_custom_fusion.3 = bf16[896,128]{1,0:T(8,128)(2,1)S(1)} fusion(s32[2048]{0:T(1024)} %get-tuple-element.120, bf16[2048,128]{1,0:T(8,128)(2,1)} %copy.99, bf16[]{:T(256)} %constant.59.clone.1), kind=kCustom, calls=%fused_computation.261 | custom fusion | flops 262144 | bytes 229888 | tf_op jit(solution)/shard_map/transpose(jvp())/scatter-add | solution.py:42
  228.4 2.8 collective-permute-start.12
  232.4 4.6 collective-permute-start.14
  238.3 11.6 %scatter_fusion = bf16[512,128]{1,0:T(8,128)(2,1)S(1)} fusion(bf16[512,128]{1,0:T(8,128)(2,1)S(1)} %slice_add_fusion.2, s32[2048]{0:T(1024)S(1)} %copy-done.73, bf16[2048,128]{1,0:T(8,128)(2,1)S(1)} %copy.100), kind=kCustom, calls=%fused_computation.16 | custom fusion | flops 262144 | bytes 1581056 | tf_op jit(solution)/shard_map/transpose(jvp())/scatter-add | solution.py:42
  251.4 1.5 constant_dynamic-update-slice_fusion.34
  255.5 1.6 constant_dynamic-update-slice_fusion.25
  264.1 3.6 stack.26
  267.7 3.2 scatter_custom_fusion.5
  273.4 1.6 fusion.194
  278.7 7.6 %gather_fusion.10 = f32[2048,128]{1,0:T(8,128)} fusion(f32[512,128]{1,0:T(8,128)S(1)} %fusion.21, s32[2048]{0:T(1024)S(1)} %copy-done.72), kind=kCustom, calls=%fused_computation.10 | custom fusion | bytes 2105344 | tf_op jit(solution)/shard_map/transpose(jvp())/gather | solution.py:54
  286.3 1.6 copy.103
  287.9 2.0 multiply_reduce_fusion.1
  290.0 1.6 fusion.161
  293.3 2.0 fusion.193
  300.0 11.9 %scatter_custom_fusion.6 = bf16[896,128]{1,0:T(8,128)(2,1)S(1)} fusion(s32[2048]{0:T(1024)} %get-tuple-element.120, bf16[2048,128]{1,0:T(8,128)(2,1)} %copy.105, bf16[]{:T(256)} %constant.59.clone.1), kind=kCustom, calls=%fused_computation.259 | custom fusion | flops 262144 | bytes 229888 | tf_op jit(solution)/shard_map/transpose(jvp())/scatter-add | solution.py:42
  314.5 11.8 %scatter_fusion.1 = bf16[512,128]{1,0:T(8,128)(2,1)S(1)} fusion(bf16[512,128]{1,0:T(8,128)(2,1)S(1)} %slice_add_fusion.1, s32[2048]{0:T(1024)} %get-tuple-element.117, bf16[2048,128]{1,0:T(8,128)(2,1)S(1)} %copy.106), kind=kCustom, calls=%fused_computation.19 | custom fusion | flops 262144 | bytes 1581056 | tf_op jit(solution)/shard_map/transpose(jvp())/scatter-add | solution.py:42
  327.3 2.8 collective-permute-start.16
  331.5 4.3 collective-permute-start.18
  342.7 1.6 constant_dynamic-update-slice_fusion.24
  351.3 3.6 stack.25
  354.9 2.9 scatter_custom_fusion.8
  361.4 1.6 fusion.196
  367.8 8.3 %gather_fusion.11 = f32[2048,128]{1,0:T(8,128)} fusion(f32[512,128]{1,0:T(8,128)S(1)} %fusion.23, s32[2048]{0:T(1024)} %get-tuple-element.119), kind=kCustom, calls=%fused_computation.11 | custom fusion | bytes 2105344 | tf_op jit(solution)/shard_map/transpose(jvp())/gather | solution.py:54
  376.1 2.6 copy.109
  378.7 2.0 multiply_reduce_fusion.2
  385.0 2.5 stack.24
  387.5 2.4 pad_maximum_fusion
  390.3 56.3 %all-reduce.3.cloned.1.call-done = f32[3,131840]{1,0:T(4,128)} async-done(((f32[3,131840]{1,0:T(4,128)}), f32[3,131840]{1,0:T(4,128)}) %all-reduce.3.cloned.1.call-update) | async-done | bytes 1582096 | tf_op jit(solution)/shard_map/psum | solution.py:8
  450.0 11.7 %scatter_custom_fusion.9 = bf16[896,128]{1,0:T(8,128)(2,1)S(1)} fusion(s32[2048]{0:T(1024)} %get-tuple-element.120, bf16[2048,384]{1,0:T(8,128)(2,1)S(1)} %convolution_convert_fusion, bf16[]{:T(256)} %constant.59.clone.1), kind=kCustom, calls=%fused_computation.171 | custom fusion | flops 262144 | bytes 754176 | tf_op jit(solution)/shard_map/transpose(jvp())/scatter-add | solution.py:42
  461.8 11.7 %scatter_custom_fusion.10 = bf16[512,128]{1,0:T(8,128)(2,1)S(1)} fusion(bf16[512,128]{1,0:T(8,128)(2,1)S(1)} %slice_add_fusion, s32[2048]{0:T(1024)} %get-tuple-element.117, bf16[2048,384]{1,0:T(8,128)(2,1)S(1)} %convolution_convert_fusion), kind=kCustom, calls=%fused_computation.169 | custom fusion | flops 262144 | bytes 655360 | tf_op jit(solution)/shard_map/transpose(jvp())/scatter-add | solution.py:42
  473.5 1.6 collective-permute-start.20
  476.5 3.4 collective-permute-start.22
  481.4 4.3 collective-permute-done.23
  485.7 2.9 scatter_custom_fusion.11
  488.6 64.0 %all-reduce.5.cloned.1.call-done = f32[3,131840]{1,0:T(4,128)} async-done(((f32[3,131840]{1,0:T(4,128)}), f32[3,131840]{1,0:T(4,128)}) %all-reduce.5.cloned.1.call-update) | async-done | bytes 1582096 | tf_op jit(solution)/shard_map/psum | solution.py:8
  552.6 1.8 fusion.167
  555.1 2.3 fusion.165
  558.1 2.2 fusion.168
  (512 shorter events, 142.0 us)
Async XLA Ops:
  7.2 21.9 %copy-start = (bf16[512,128]{1,0:T(8,128)(2,1)S(1)}, bf16[512,128]{1,0:T(8,128)(2,1)}, u32[]{:S(2)}) copy-start(bf16[512,128]{1,0:T(8,128)(2,1)} %param.19) | copy-start | bytes 393220
  7.2 17.7 %copy-start.115 = (f32[3,128]{1,0:T(4,128)S(1)}, f32[3,128]{1,0:T(4,128)}, u32[]{:S(2)}) copy-start(f32[3,128]{1,0:T(4,128)} %param.29) | copy-start | bytes 4612
  7.2 18.2 %copy-start.116 = (f32[3,128]{1,0:T(4,128)S(1)}, f32[3,128]{1,0:T(4,128)}, u32[]{:S(2)}) copy-start(f32[3,128]{1,0:T(4,128)} %param.30) | copy-start | bytes 4612
  7.2 18.8 %copy-start.117 = (f32[3,128]{1,0:T(4,128)S(1)}, f32[3,128]{1,0:T(4,128)}, u32[]{:S(2)}) copy-start(f32[3,128]{1,0:T(4,128)} %param.32) | copy-start | bytes 4612
  7.2 19.4 %copy-start.118 = (f32[3,128]{1,0:T(4,128)S(1)}, f32[3,128]{1,0:T(4,128)}, u32[]{:S(2)}) copy-start(f32[3,128]{1,0:T(4,128)} %param.34) | copy-start | bytes 4612
  7.2 19.9 %copy-start.119 = (f32[3,128]{1,0:T(4,128)S(1)}, f32[3,128]{1,0:T(4,128)}, u32[]{:S(2)}) copy-start(f32[3,128]{1,0:T(4,128)} %param.35) | copy-start | bytes 4612
  7.3 20.5 %copy-start.103 = (s32[2048]{0:T(1024)S(1)}, s32[2048]{0:T(1024)}, u32[]{:S(2)}) copy-start(s32[2048]{0:T(1024)} %param.21) | copy-start | bytes 24580
  7.3 21.1 %copy-start.91 = (s32[2048]{0:T(1024)S(1)}, s32[2048]{0:T(1024)}, u32[]{:S(2)}) copy-start(s32[2048]{0:T(1024)} %param.22) | copy-start | bytes 24580
  7.3 21.7 %copy-start.20 = (bf16[2048,128]{1,0:T(8,128)(2,1)S(1)}, bf16[2048,128]{1,0:T(8,128)(2,1)}, u32[]{:S(2)}) copy-start(bf16[2048,128]{1,0:T(8,128)(2,1)} %param.20) | copy-start | bytes 1572868
  7.3 439.3 %all-reduce.3.cloned.1.call-start = ((), (), s32[]{:S(2)}) async-start(), calls=%async_computation | async-start | bytes 4218880 | tf_op jit(solution)/shard_map/psum | solution.py:8
  8.1 20.9 %copy-start.104 = (s32[384]{0:T(512)}, s32[384]{0:T(512)S(1)}, u32[]{:S(2)}) copy-start(s32[384]{0:T(512)S(1)} %compare_select_fusion.2) | copy-start | bytes 4612
  9.2 20.9 %copy-start.26 = (bf16[512,128]{0,1:T(8,128)(2,1)}, bf16[512,128]{0,1:T(8,128)(2,1)S(1)}, u32[]{:S(2)}) copy-start(bf16[512,128]{0,1:T(8,128)(2,1)S(1)} %copy.72) | copy-start | bytes 393220
  9.3 20.8 %copy-start.113 = (s32[512]{0:T(512)S(1)}, s32[512]{0:T(512)}, u32[]{:S(2)}) copy-start(s32[512]{0:T(512)} %param.24) | copy-start | bytes 6148
  9.3 20.8 %copy-start.105 = (s32[2048]{0:T(1024)S(1)}, s32[2048]{0:T(1024)}, u32[]{:S(2)}) copy-start(s32[2048]{0:T(1024)} %param.23) | copy-start | bytes 24580
  9.3 20.8 %copy-start.59 = (f32[3,128,128]{2,1,0:T(8,128)S(1)}, f32[3,128,128]{2,1,0:T(8,128)}, u32[]{:S(2)}) copy-start(f32[3,128,128]{2,1,0:T(8,128)} %param.28) | copy-start | bytes 589828
  10.8 20.0 %copy-start.60 = (f32[3,128,128]{2,1,0:T(8,128)S(1)}, f32[3,128,128]{2,1,0:T(8,128)}, u32[]{:S(2)}) copy-start(f32[3,128,128]{2,1,0:T(8,128)} %param.33) | copy-start | bytes 589828
  11.4 30.9 %collective-permute-start.1 = (bf16[64,128]{1,0:T(8,128)(2,1)}, bf16[64,128]{1,0:T(8,128)(2,1)}, u32[]{:S(2)}, u32[]{:S(2)}) collective-permute-start(bf16[64,128]{1,0:T(8,128)(2,1)} %get-tuple-element.115), channel_id=1, source_target_pairs={{1,0},{2,1},{3,2},{5,4},{6,5},{7,6},{9,8},{10,9},{11,10},{13,12},{... | collective-permute-start | bytes 49160 | tf_op jit(solution)/shard_map/ppermute | solution.py:15
  12.7 28.9 %collective-permute-start = (bf16[64,128]{1,0:T(8,128)(2,1)}, bf16[64,128]{1,0:T(8,128)(2,1)}, u32[]{:S(2)}, u32[]{:S(2)}) collective-permute-start(bf16[64,128]{1,0:T(8,128)(2,1)} %get-tuple-element.116), channel_id=1, source_target_pairs={{0,1},{1,2},{2,3},{4,5},{5,6},{6,7},{8,9},{9,10},{10,11},{12,13},{... | collective-permute-start | bytes 49160 | tf_op jit(solution)/shard_map/ppermute | solution.py:15
  16.9 26.8 %collective-permute-start.3 = (bf16[128,128]{1,0:T(8,128)(2,1)}, bf16[128,128]{1,0:T(8,128)(2,1)}, u32[]{:S(2)}, u32[]{:S(2)}) collective-permute-start(bf16[128,128]{1,0:T(8,128)(2,1)} %get-tuple-element.113), channel_id=1, source_target_pairs={{4,0},{8,4},{12,8},{16,12},{20,16},{24,20},{28,24},{5,1},{9,5},{13... | collective-permute-start | bytes 98312 | tf_op jit(solution)/shard_map/ppermute | solution.py:15
  18.2 24.8 %collective-permute-start.2 = (bf16[128,128]{1,0:T(8,128)(2,1)}, bf16[128,128]{1,0:T(8,128)(2,1)}, u32[]{:S(2)}, u32[]{:S(2)}) collective-permute-start(bf16[128,128]{1,0:T(8,128)(2,1)} %get-tuple-element.114), channel_id=1, source_target_pairs={{0,4},{4,8},{8,12},{12,16},{16,20},{20,24},{24,28},{1,5},{5,9},{9,... | collective-permute-start | bytes 98312 | tf_op jit(solution)/shard_map/ppermute | solution.py:15
  33.0 35.1 %copy-start.42 = (bf16[3,256,128]{2,1,0:T(8,128)(2,1)}, bf16[3,256,128]{2,1,0:T(8,128)(2,1)S(1)}, u32[]{:S(2)}) copy-start(bf16[3,256,128]{2,1,0:T(8,128)(2,1)S(1)} %convert.42) | copy-start | bytes 589828
  69.6 21.1 %copy-start.95 = (f32[512]{0:T(512)}, f32[512]{0:T(512)S(1)}, u32[]{:S(2)}) copy-start(f32[512]{0:T(512)S(1)} %multiply_reduce_fusion.17) | copy-start | bytes 6148
  69.6 21.1 %copy-start.86 = (f32[512]{0:T(512)}, f32[512]{0:T(512)S(1)}, u32[]{:S(2)}) copy-start(f32[512]{0:T(512)S(1)} %fusion.145) | copy-start | bytes 6148
  70.6 21.7 %copy-start.28 = (bf16[512,128]{0,1:T(8,128)(2,1)}, bf16[512,128]{0,1:T(8,128)(2,1)S(1)}, u32[]{:S(2)}) copy-start(bf16[512,128]{0,1:T(8,128)(2,1)S(1)} %get-tuple-element.144) | copy-start | bytes 393220
  72.4 19.4 %collective-permute-start.7 = (bf16[128,128]{0,1:T(8,128)(2,1)S(1)}, bf16[128,128]{0,1:T(8,128)(2,1)}, u32[]{:S(2)}, u32[]{:S(2)}) collective-permute-start(bf16[128,128]{0,1:T(8,128)(2,1)S(1)} %get-tuple-element.109), channel_id=1, source_target_pairs={{4,0},{8,4},{12,8},{16,12},{20,16},{24,20},{28,24},{5,1},{9,5},{13... | collective-permute-start | bytes 98312 | tf_op jit(solution)/shard_map/ppermute | solution.py:15
  73.7 18.7 %collective-permute-start.6 = (bf16[128,128]{0,1:T(8,128)(2,1)S(1)}, bf16[128,128]{0,1:T(8,128)(2,1)}, u32[]{:S(2)}, u32[]{:S(2)}) collective-permute-start(bf16[128,128]{0,1:T(8,128)(2,1)S(1)} %get-tuple-element.110), channel_id=1, source_target_pairs={{0,4},{4,8},{8,12},{12,16},{16,20},{20,24},{24,28},{1,5},{5,9},{9,... | collective-permute-start | bytes 98312 | tf_op jit(solution)/shard_map/ppermute | solution.py:15
  79.8 12.0 %collective-permute-start.5 = (bf16[64,128]{0,1:T(8,128)(2,1)}, bf16[64,128]{0,1:T(8,128)(2,1)S(1)}, u32[]{:S(2)}, u32[]{:S(2)}) collective-permute-start(bf16[64,128]{0,1:T(8,128)(2,1)} %get-tuple-element.111), channel_id=1, source_target_pairs={{1,0},{2,1},{3,2},{5,4},{6,5},{7,6},{9,8},{10,9},{11,10},{13,12},{... | collective-permute-start | bytes 49160 | tf_op jit(solution)/shard_map/ppermute | solution.py:15
  81.0 10.7 %collective-permute-start.4 = (bf16[64,128]{0,1:T(8,128)(2,1)S(1)}, bf16[64,128]{0,1:T(8,128)(2,1)S(1)}, u32[]{:S(2)}, u32[]{:S(2)}) collective-permute-start(bf16[64,128]{0,1:T(8,128)(2,1)S(1)} %get-tuple-element.112), channel_id=1, source_target_pairs={{0,1},{1,2},{2,3},{4,5},{5,6},{6,7},{8,9},{9,10},{10,11},{12,13},{... | collective-permute-start | bytes 49160 | tf_op jit(solution)/shard_map/ppermute | solution.py:15
  124.6 22.8 %copy-start.15 = (f32[512,128]{0,1:T(8,128)}, f32[512,128]{0,1:T(8,128)S(1)}, u32[]{:S(2)}) copy-start(f32[512,128]{0,1:T(8,128)S(1)} %get-tuple-element.151) | copy-start | bytes 786436
  124.6 23.8 %copy-start.33 = (bf16[512,128]{0,1:T(8,128)(2,1)}, bf16[512,128]{0,1:T(8,128)(2,1)S(1)}, u32[]{:S(2)}) copy-start(bf16[512,128]{0,1:T(8,128)(2,1)S(1)} %get-tuple-element.150) | copy-start | bytes 393220
  127.7 20.8 %collective-permute-start.9 = (bf16[64,128]{0,1:T(8,128)(2,1)}, bf16[64,128]{0,1:T(8,128)(2,1)}, u32[]{:S(2)}, u32[]{:S(2)}) collective-permute-start(bf16[64,128]{0,1:T(8,128)(2,1)} %get-tuple-element.107), channel_id=1, source_target_pairs={{1,0},{2,1},{3,2},{5,4},{6,5},{7,6},{9,8},{10,9},{11,10},{13,12},{... | collective-permute-start | bytes 49160 | tf_op jit(solution)/shard_map/ppermute | solution.py:15
  128.9 19.5 %collective-permute-start.8 = (bf16[64,128]{0,1:T(8,128)(2,1)}, bf16[64,128]{0,1:T(8,128)(2,1)}, u32[]{:S(2)}, u32[]{:S(2)}) collective-permute-start(bf16[64,128]{0,1:T(8,128)(2,1)} %get-tuple-element.108), channel_id=1, source_target_pairs={{0,1},{1,2},{2,3},{4,5},{5,6},{6,7},{8,9},{9,10},{10,11},{12,13},{... | collective-permute-start | bytes 49160 | tf_op jit(solution)/shard_map/ppermute | solution.py:15
  133.4 15.0 %collective-permute-start.11 = (bf16[128,128]{0,1:T(8,128)(2,1)}, bf16[128,128]{0,1:T(8,128)(2,1)}, u32[]{:S(2)}, u32[]{:S(2)}) collective-permute-start(bf16[128,128]{0,1:T(8,128)(2,1)} %get-tuple-element.105), channel_id=1, source_target_pairs={{4,0},{8,4},{12,8},{16,12},{20,16},{24,20},{28,24},{5,1},{9,5},{13... | collective-permute-start | bytes 98312 | tf_op jit(solution)/shard_map/ppermute | solution.py:15
  134.7 13.8 %collective-permute-start.10 = (bf16[128,128]{0,1:T(8,128)(2,1)}, bf16[128,128]{0,1:T(8,128)(2,1)}, u32[]{:S(2)}, u32[]{:S(2)}) collective-permute-start(bf16[128,128]{0,1:T(8,128)(2,1)} %get-tuple-element.106), channel_id=1, source_target_pairs={{0,4},{4,8},{8,12},{12,16},{16,20},{20,24},{24,28},{1,5},{5,9},{9,... | collective-permute-start | bytes 98312 | tf_op jit(solution)/shard_map/ppermute | solution.py:15
  140.1 45.5 %copy-start.5 = (f32[512,128]{0,1:T(8,128)}, f32[512,128]{0,1:T(8,128)S(1)}, u32[]{:S(2)}) copy-start(f32[512,128]{0,1:T(8,128)S(1)} %copy.95) | copy-start | bytes 786436
  213.0 25.3 %copy-start.73 = (s32[2048]{0:T(1024)S(1)}, s32[2048]{0:T(1024)}, u32[]{:S(2)}) copy-start(s32[2048]{0:T(1024)} %get-tuple-element.117) | copy-start | bytes 24580
  228.4 39.3 %collective-permute-start.12 = (bf16[64,128]{1,0:T(8,128)(2,1)}, bf16[64,128]{1,0:T(8,128)(2,1)S(1)}, u32[]{:S(2)}, u32[]{:S(2)}) collective-permute-start(bf16[64,128]{1,0:T(8,128)(2,1)} %get-tuple-element.101), channel_id=1, source_target_pairs={{0,1},{1,2},{2,3},{4,5},{5,6},{6,7},{8,9},{9,10},{10,11},{12,13},{... | collective-permute-start | bytes 49160 | tf_op jit(solution)/shard_map/ppermute | solution.py:15
  231.1 36.5 %collective-permute-start.13 = (bf16[64,128]{1,0:T(8,128)(2,1)}, bf16[64,128]{1,0:T(8,128)(2,1)}, u32[]{:S(2)}, u32[]{:S(2)}) collective-permute-start(bf16[64,128]{1,0:T(8,128)(2,1)} %get-tuple-element.102), channel_id=1, source_target_pairs={{1,0},{2,1},{3,2},{5,4},{6,5},{7,6},{9,8},{10,9},{11,10},{13,12},{... | collective-permute-start | bytes 49160 | tf_op jit(solution)/shard_map/ppermute | solution.py:15
  232.4 35.2 %collective-permute-start.14 = (bf16[128,128]{1,0:T(8,128)(2,1)}, bf16[128,128]{1,0:T(8,128)(2,1)}, u32[]{:S(2)}, u32[]{:S(2)}) collective-permute-start(bf16[128,128]{1,0:T(8,128)(2,1)} %get-tuple-element.103), channel_id=1, source_target_pairs={{0,4},{4,8},{8,12},{12,16},{16,20},{20,24},{24,28},{1,5},{5,9},{9,... | collective-permute-start | bytes 98312 | tf_op jit(solution)/shard_map/ppermute | solution.py:15
  237.0 30.7 %collective-permute-start.15 = (bf16[128,128]{1,0:T(8,128)(2,1)S(1)}, bf16[128,128]{1,0:T(8,128)(2,1)}, u32[]{:S(2)}, u32[]{:S(2)}) collective-permute-start(bf16[128,128]{1,0:T(8,128)(2,1)S(1)} %get-tuple-element.104), channel_id=1, source_target_pairs={{4,0},{8,4},{12,8},{16,12},{20,16},{24,20},{28,24},{5,1},{9,5},{13... | collective-permute-start | bytes 98312 | tf_op jit(solution)/shard_map/ppermute | solution.py:15
  238.3 17.2 %copy-start.70 = (f32[32768]{0:T(1024)S(1)}, f32[32768]{0:T(1024)}, u32[]{:S(2)}) copy-start(f32[32768]{0:T(1024)} %fusion.25) | copy-start | bytes 393220
  238.3 24.2 %copy-start.50 = (f32[16384]{0:T(1024)S(1)}, f32[16384]{0:T(1024)}, u32[]{:S(2)}) copy-start(f32[16384]{0:T(1024)} %fusion.37) | copy-start | bytes 196612
  250.0 21.0 %copy-start.14 = (f32[512,128]{0,1:T(8,128)S(1)}, f32[512,128]{0,1:T(8,128)}, u32[]{:S(2)}) copy-start(f32[512,128]{0,1:T(8,128)} %copy-done.13) | copy-start | bytes 786436
  250.0 21.0 %copy-start.85 = (f32[512]{0:T(512)S(1)}, f32[512]{0:T(512)}, u32[]{:S(2)}) copy-start(f32[512]{0:T(512)} %copy-done.84) | copy-start | bytes 6148
  250.0 21.0 %copy-start.90 = (f32[512]{0:T(512)S(1)}, f32[512]{0:T(512)}, u32[]{:S(2)}) copy-start(f32[512]{0:T(512)} %copy-done.89) | copy-start | bytes 6148
  250.0 21.0 %copy-start.107 = (f32[128]{0:T(128)S(1)}, f32[128]{0:T(128)}, u32[]{:S(2)}) copy-start(f32[128]{0:T(128)} %get-tuple-element.124) | copy-start | bytes 1540
  251.4 20.3 %copy-start.97 = (f32[512]{0:T(512)S(1)}, f32[512]{0:T(512)}, u32[]{:S(2)}) copy-start(f32[512]{0:T(512)} %copy-done.96) | copy-start | bytes 6148
  326.3 31.6 %copy-start.10 = (f32[512,128]{0,1:T(8,128)S(1)}, f32[512,128]{0,1:T(8,128)}, u32[]{:S(2)}) copy-start(f32[512,128]{0,1:T(8,128)} %copy-done.9) | copy-start | bytes 786436
  327.3 27.5 %collective-permute-start.16 = (bf16[64,128]{1,0:T(8,128)(2,1)}, bf16[64,128]{1,0:T(8,128)(2,1)S(1)}, u32[]{:S(2)}, u32[]{:S(2)}) collective-permute-start(bf16[64,128]{1,0:T(8,128)(2,1)} %get-tuple-element.97), channel_id=1, source_target_pairs={{0,1},{1,2},{2,3},{4,5},{5,6},{6,7},{8,9},{9,10},{10,11},{12,13},{... | collective-permute-start | bytes 49160 | tf_op jit(solution)/shard_map/ppermute | solution.py:15
  330.2 24.7 %collective-permute-start.17 = (bf16[64,128]{1,0:T(8,128)(2,1)}, bf16[64,128]{1,0:T(8,128)(2,1)S(1)}, u32[]{:S(2)}, u32[]{:S(2)}) collective-permute-start(bf16[64,128]{1,0:T(8,128)(2,1)} %get-tuple-element.98), channel_id=1, source_target_pairs={{1,0},{2,1},{3,2},{5,4},{6,5},{7,6},{9,8},{10,9},{11,10},{13,12},{... | collective-permute-start | bytes 49160 | tf_op jit(solution)/shard_map/ppermute | solution.py:15
  331.5 23.4 %collective-permute-start.18 = (bf16[128,128]{1,0:T(8,128)(2,1)}, bf16[128,128]{1,0:T(8,128)(2,1)S(1)}, u32[]{:S(2)}, u32[]{:S(2)}) collective-permute-start(bf16[128,128]{1,0:T(8,128)(2,1)} %get-tuple-element.99), channel_id=1, source_target_pairs={{0,4},{4,8},{8,12},{12,16},{16,20},{20,24},{24,28},{1,5},{5,9},{9,... | collective-permute-start | bytes 98312 | tf_op jit(solution)/shard_map/ppermute | solution.py:15
  335.7 19.1 %collective-permute-start.19 = (bf16[128,128]{1,0:T(8,128)(2,1)}, bf16[128,128]{1,0:T(8,128)(2,1)S(1)}, u32[]{:S(2)}, u32[]{:S(2)}) collective-permute-start(bf16[128,128]{1,0:T(8,128)(2,1)} %get-tuple-element.100), channel_id=1, source_target_pairs={{4,0},{8,4},{12,8},{16,12},{20,16},{24,20},{28,24},{5,1},{9,5},{13... | collective-permute-start | bytes 98312 | tf_op jit(solution)/shard_map/ppermute | solution.py:15
  389.9 56.7 %copy-start.12 = (f32[512,128]{0,1:T(8,128)S(1)}, f32[512,128]{0,1:T(8,128)}, u32[]{:S(2)}) copy-start(f32[512,128]{0,1:T(8,128)} %copy-done.11) | copy-start | bytes 786436
  389.9 56.7 %copy-start.16 = (f32[512,128]{0,1:T(8,128)S(1)}, f32[512,128]{0,1:T(8,128)}, u32[]{:S(2)}) copy-start(f32[512,128]{0,1:T(8,128)} %copy-done.15) | copy-start | bytes 786436
  389.9 56.7 %copy-start.25 = (bf16[512,128]{0,1:T(8,128)(2,1)S(1)}, bf16[512,128]{0,1:T(8,128)(2,1)}, u32[]{:S(2)}) copy-start(bf16[512,128]{0,1:T(8,128)(2,1)} %copy.93) | copy-start | bytes 393220
  389.9 56.7 %copy-start.83 = (f32[512]{0:T(512)S(1)}, f32[512]{0:T(512)}, u32[]{:S(2)}) copy-start(f32[512]{0:T(512)} %copy-done.82) | copy-start | bytes 6148
  390.0 56.7 %copy-start.88 = (f32[512]{0:T(512)S(1)}, f32[512]{0:T(512)}, u32[]{:S(2)}) copy-start(f32[512]{0:T(512)} %copy-done.87) | copy-start | bytes 6148
  390.0 56.7 %copy-start.99 = (f32[128]{0:T(128)S(1)}, f32[128]{0:T(128)}, u32[]{:S(2)}) copy-start(f32[128]{0:T(128)} %get-tuple-element.122) | copy-start | bytes 1540
  390.0 162.6 %all-reduce.5.cloned.1.call-start = ((), (), s32[]{:S(2)}) async-start(), calls=%async_computation.1 | async-start | bytes 4218880 | tf_op jit(solution)/shard_map/psum | solution.py:8
  473.5 7.7 %collective-permute-start.20 = (bf16[64,128]{1,0:T(8,128)(2,1)S(1)}, bf16[64,128]{1,0:T(8,128)(2,1)S(1)}, u32[]{:S(2)}, u32[]{:S(2)}) collective-permute-start(bf16[64,128]{1,0:T(8,128)(2,1)S(1)} %get-tuple-element.93), channel_id=1, source_target_pairs={{0,1},{1,2},{2,3},{4,5},{5,6},{6,7},{8,9},{9,10},{10,11},{12,13},{... | collective-permute-start | bytes 49160 | tf_op jit(solution)/shard_map/ppermute | solution.py:15
  475.2 6.1 %collective-permute-start.21 = (bf16[64,128]{1,0:T(8,128)(2,1)S(1)}, bf16[64,128]{1,0:T(8,128)(2,1)S(1)}, u32[]{:S(2)}, u32[]{:S(2)}) collective-permute-start(bf16[64,128]{1,0:T(8,128)(2,1)S(1)} %get-tuple-element.94), channel_id=1, source_target_pairs={{1,0},{2,1},{3,2},{5,4},{6,5},{7,6},{9,8},{10,9},{11,10},{13,12},{... | collective-permute-start | bytes 49160 | tf_op jit(solution)/shard_map/ppermute | solution.py:15
  476.5 5.0 collective-permute-start.22
  479.9 5.8 %collective-permute-start.23 = (bf16[128,128]{1,0:T(8,128)(2,1)S(1)}, bf16[128,128]{1,0:T(8,128)(2,1)S(1)}, u32[]{:S(2)}, u32[]{:S(2)}) collective-permute-start(bf16[128,128]{1,0:T(8,128)(2,1)S(1)} %get-tuple-element.96), channel_id=1, source_target_pairs={{4,0},{8,4},{12,8},{16,12},{20,16},{24,20},{28,24},{5,1},{9,5},{13... | collective-permute-start | bytes 98312 | tf_op jit(solution)/shard_map/ppermute | solution.py:15
  488.6 69.5 %copy-start.52 = (f32[512,128]{1,0:T(8,128)}, f32[512,128]{1,0:T(8,128)S(1)}, u32[]{:S(2)}) copy-start(f32[512,128]{1,0:T(8,128)S(1)} %scatter_custom_fusion.11) | copy-start | bytes 786436
  (102 other events, 439.5 us)
Sparse Core Ops, SparseCore 0:
  390.0 56.5 all-reduce.2
  450.2 102.3 all-reduce.4
